TPU v7x, 32 devices: a whole 2x2x4 slice. The times are simulated.
32 devices in a mesh: row: 8 (over y, x, core), col: 4 (over z).
Axes of the slice: x: 2, y: 2, z: 4, core: 2. Of those that a mesh axis runs over, the one named last changes fastest.
Arguments:
- inverse_blocks: bfloat16 [8, 384, 256, 256], P('row', 'col'), may hold values from -6 to 6
- inverse_rows: int32 [8, 384], P('row', 'col'), may hold values from 0 to 95, as said below
- inverse_cols: int32 [8, 384], P('row', 'col'), may hold values from 0 to 95, as said below
- inverse_count: int32 [8, 4], P('row', 'col'), may hold values from 1 to 96, as said below
- panel_rows: int32 [16], replicated, may hold values from -1 to 95, as said below
- lower_old: bfloat16 [3, 16, 256, 256], P(None, 'row'), may hold values from -0.038085938 to 0.038085938
- lower_new: bfloat16 [3, 3, 256, 256], replicated, may hold values from -0.375 to 0.375
- diag_inverse: float32 [3, 256, 256], replicated, may hold values from -6 to 6
Outputs:
- panel_inverse: bfloat16 [3, 16, 256, 256], P(None, 'row', 'col')
- supernode_inverse: float32 [3, 3, 256, 256], replicated
Inputs may be any that keep to these rules, and one draw needn't show every extreme that they name: `panel_rows`: for each row index r in order, 2 entries: distinct block rows congruent to r modulo the number of row indices, at least one, then -1 in the empty slots; some row index fills all 2 in every draw. `inverse_rows`: on row index r every slot names one of the panel rows of r, padding slots too. `inverse_cols`: on column index c every slot names a block column congruent to c modulo the number of column indices; positions may repeat, and repeated blocks add. `inverse_count`: slots 0 to count - 1 of a device's lists are live, the rest padding; one device reaches 96 in every draw.
All inputs are finite; a program needn't handle non-finite values.
Results may differ from a plain program's by a relative error of at most 0.0045.
Values may be sent and summed in bfloat16 or wider, within the bound.
No kernel may reach another device: no remote copies, remote signals or barrier semaphores. Data moves between devices by JAX's collectives and lax.ppermute only.
A program may use at most 128 MiB of HBM per device.

v0:
```python
import jax
import jax.numpy as jnp
from jax import lax
from jax.sharding import PartitionSpec as P

exact_mode = lax.Precision.HIGHEST
group_size = 8


def partner_2(value, axis, distance):
    mask = 2**distance
    pairs = [(source, source ^ mask) for source in range(lax.axis_size(axis))]
    return lax.ppermute(value, axis, pairs)


def linked(blocks_new, left_node, right_node):
    if left_node == right_node:
        return blocks_new[left_node, left_node]
    if right_node > left_node:
        return blocks_new[right_node, left_node]
    return blocks_new[left_node, right_node].T


def per_device(
    inverse_blocks,
    inverse_rows,
    inverse_cols,
    inverse_count,
    panel_rows,
    lower_old,
    lower_new,
    diag_inverse,
):
    blocks = inverse_blocks[0]
    stored_rows = inverse_rows[0]
    stored_cols = inverse_cols[0]
    stored_count = inverse_count[0, 0]
    supernodes = lower_old.shape[0]
    slot_count = lower_old.shape[1]
    block_width = blocks.shape[-1]
    row_devs = lax.axis_size("row")
    col_devs = lax.axis_size("col")
    row_me = lax.axis_index("row")
    col_me = lax.axis_index("col")
    own_rows = lax.dynamic_slice_in_dim(panel_rows, row_me * slot_count, slot_count)
    holding = lower_old
    for bit_index in range(col_devs.bit_length() - 1):
        partner = partner_2(holding, "row", bit_index)
        differ = row_me >> bit_index & 1 != col_me >> bit_index & 1
        holding = jnp.where(differ, partner, holding)
    for bit_index in range(col_devs.bit_length() - 1, row_devs.bit_length() - 1):
        partner = partner_2(holding, "row", bit_index)
        upper_half = row_me >> bit_index & 1 == 1
        holding = jnp.where(
            upper_half,
            jnp.concatenate([partner, holding], axis=1),
            jnp.concatenate([holding, partner], axis=1),
        )
    candidates = holding
    sources = jnp.arange(row_devs // col_devs, dtype=jnp.int32) * col_devs + col_me
    cand_rows = panel_rows.reshape(row_devs, slot_count)[sources].reshape(-1)
    cand_index = jnp.arange(cand_rows.shape[0], dtype=jnp.int32)

    def accumulate(group_index, running):
        offset = group_index * group_size
        block_part = lax.dynamic_slice_in_dim(blocks, offset, group_size)
        row_part = lax.dynamic_slice_in_dim(stored_rows, offset, group_size)
        col_part = lax.dynamic_slice_in_dim(stored_cols, offset, group_size)
        is_live = offset + jnp.arange(group_size, dtype=jnp.int32) < stored_count
        matches = col_part[:, None] == cand_rows[None, :]
        present = jnp.any(matches, axis=1) & is_live
        position = jnp.sum(jnp.where(matches, cand_index[None, :], 0), axis=1)
        factors = jnp.take(candidates, position, axis=1)
        products = jnp.einsum(
            "kab,skbc->skac", block_part, factors, preferred_element_type=jnp.float32
        )
        target = ((row_part[:, None] == own_rows[None, :]) & present[:, None]).astype(jnp.float32)
        return running + jnp.einsum("ks,tkac->tsac", target, products, precision=exact_mode)

    partial_value = lax.fori_loop(
        0,
        (stored_count + group_size - 1) // group_size,
        accumulate,
        jnp.zeros((supernodes, slot_count, block_width, block_width), jnp.float32),
    )
    share_rows = block_width // col_devs
    base_part = lax.psum(partial_value, "col")
    lower_links = lower_new.astype(jnp.float32)
    panels = []
    blocks_new = {}
    for node in range(supernodes):
        running = base_part[node]
        for earlier in range(node):
            running = running + jnp.einsum(
                "sab,bc->sac",
                panels[earlier],
                lower_new[node, earlier],
                preferred_element_type=jnp.float32,
            )
        current = (-running).astype(jnp.bfloat16)
        lower_step = lower_old[node]
        term_list = [
            jnp.einsum(
                "sab,sac->bc", panels[earlier], lower_step, preferred_element_type=jnp.float32
            )
            for earlier in range(node)
        ]
        term_list.append(
            jnp.einsum("sab,sac->bc", lower_step, current, preferred_element_type=jnp.float32)
        )
        summed = lax.psum(jnp.stack(term_list), "row")
        for earlier in range(node):
            crossed = summed[earlier]
            for another in range(node):
                crossed = crossed + jnp.dot(
                    linked(blocks_new, earlier, another),
                    lower_links[node, another],
                    precision=exact_mode,
                )
            blocks_new[node, earlier] = -crossed
        diagonal_block = diag_inverse[node] - summed[node]
        for earlier in range(node):
            diagonal_block = diagonal_block - jnp.dot(
                lower_links[node, earlier].T, blocks_new[node, earlier], precision=exact_mode
            )
        blocks_new[node, node] = diagonal_block
        panels.append(current)
    stacked = jnp.stack(panels)
    panel_inverse = lax.dynamic_slice_in_dim(stacked, col_me * share_rows, share_rows, 2)
    empty_block = jnp.zeros((block_width, block_width), jnp.float32)
    supernode_inverse = jnp.stack(
        [
            jnp.stack(
                [
                    blocks_new[node, earlier] if earlier <= node else empty_block
                    for earlier in range(supernodes)
                ]
            )
            for node in range(supernodes)
        ]
    )
    return (panel_inverse, supernode_inverse)


def solution(mesh):
    placed = (
        P("row", "col", None, None),
        P("row", "col"),
        P("row", "col"),
        P("row", "col"),
        P(),
        P(None, "row", None, None),
        P(),
        P(),
    )
    return jax.shard_map(
        per_device,
        mesh=mesh,
        in_specs=placed,
        out_specs=(P(None, "row", "col", None), P()),
        check_vma=False,
    )
```

profile of v0, /device:TPU:0, one launch (start us, length us, event | category | flops | bytes accessed | tf_op | source)
XLA Modules:
  0.0 490.5 jit_solution(17268165076970064919)
XLA Ops:
  7.8 2.1 collective-permute-done
  9.9 1.2 broadcast_select_fusion
  11.1 2.9 collective-permute-start.1
  14.0 16.7 %collective-permute-done.1 = bf16[3,2,256,256]{3,2,1,0:T(8,128)(2,1)S(1)} collective-permute-done((bf16[3,2,256,256]{3,2,1,0:T(8,128)(2,1)S(1)}, bf16[3,2,256,256]{3,2,1,0:T(8,128)(2,1)S(1)}, u32[]{:S(2)}, u32[]{:S(2)}) %collective-permute-start.1) | collective-permute-done | bytes 786464 | tf_op jit(solution)/shard_map/ppermute | solution.py:13
  30.8 1.8 collective-permute-start.2
  34.2 14.6 %collective-permute-done.2 = bf16[3,2,256,256]{3,2,1,0:T(8,128)(2,1)S(1)} collective-permute-done((bf16[3,2,256,256]{3,2,1,0:T(8,128)(2,1)S(1)}, bf16[3,2,256,256]{3,2,1,0:T(8,128)(2,1)S(1)}, u32[]{:S(2)}, u32[]{:S(2)}) %collective-permute-start.2) | collective-permute-done | bytes 786464 | tf_op jit(solution)/shard_map/ppermute | solution.py:13
  48.8 1.4 maximum_select_fusion
  50.2 1.5 broadcast_in_dim.31
  51.8 47.7 %while.12 = (s32[]{:T(128)}, f32[3,2,256,256]{3,1,2,0:T(2,128)}, s32[]{:T(128)}, s32[96]{0:T(128)S(1)}, s32[2,2]{1,0:T(2,128)}, /*index=5*/bf16[3,4,256,256]{3,2...) while((s32[]{:T(128)}, f32[3,2,256,256]{3,1,2,0:T(2,128)}, ...), condition=%wide.wide.region_3.4_spmd.clone, body=%wide.wide.region_0.3_spmd.clone.sunk | while | flops 845022464 | bytes 51385088 | solution.py:80
  51.9 2.2 gather_fusion
  54.1 5.1 %fusion.112 = f32[3,8,256,256]{2,3,0,1:T(8,128)} fusion(bf16[8,3,256,256]{3,2,1,0:T(8,128)(2,1)S(1)} %gather_fusion, pred[8]{0:T(512)(128)(4,1)S(1)} %compare_and_fusion.6, bf16[96,256,256]{2,1,0:T(8,128)(2,1)} %get-tuple-element.263, s32[]{:T(128)S(6)} %select_n.126), kind=kOutput, calls=%fused_computation.7.clone.clone.1 | convolution fusion | flops 806879232 | bytes 10485772 | tf_op jit(solution)/shard_map/while/body/kab,skbc->skac/dot_general | solution.py:74
  59.2 6.8 %copy.94 = f32[3,8,256,256]{3,1,2,0:T(8,128)} copy(f32[3,8,256,256]{2,3,0,1:T(8,128)} %fusion.112) | data formatting | bytes 12582912 | tf_op jit(solution)/shard_map/while/body/kab,skbc->skac/transpose | solution.py:74
  66.8 7.6 %bitcast_add_fusion.3 = f32[3,2,256,256]{3,1,2,0:T(2,128)S(1)} fusion(f32[3,2,256,256]{3,1,2,0:T(2,128)S(1)} %copy-done, f32[3,8,256,256]{3,1,2,0:T(8,128)} %copy.94, pred[8]{0:T(512)(128)(4,1)S(1)} %compare_and_fusion.7, s32[8]{0:T(128)S(1)} %dynamic_slice.46, s32[2]{0:T(128)S(1)} %get-tuple-element.265), kind=kOutput, calls=%fused_computation.8.clone.clone.1 | convolution fusion | flops 38141984 | bytes 9437232 | tf_op jit(solution)/shard_map/while/body/ks,tkac->tsac/dot_general | solution.py:78
  74.5 1.1 copy-done.1
  75.8 2.2 gather_fusion
  77.9 5.1 %fusion.112 = f32[3,8,256,256]{2,3,0,1:T(8,128)} fusion(bf16[8,3,256,256]{3,2,1,0:T(8,128)(2,1)S(1)} %gather_fusion, pred[8]{0:T(512)(128)(4,1)S(1)} %compare_and_fusion.6, bf16[96,256,256]{2,1,0:T(8,128)(2,1)} %get-tuple-element.263, s32[]{:T(128)S(6)} %select_n.126), kind=kOutput, calls=%fused_computation.7.clone.clone.1 | convolution fusion | flops 806879232 | bytes 10485772 | tf_op jit(solution)/shard_map/while/body/kab,skbc->skac/dot_general | solution.py:74
  83.1 6.8 %copy.94 = f32[3,8,256,256]{3,1,2,0:T(8,128)} copy(f32[3,8,256,256]{2,3,0,1:T(8,128)} %fusion.112) | data formatting | bytes 12582912 | tf_op jit(solution)/shard_map/while/body/kab,skbc->skac/transpose | solution.py:74
  90.7 7.6 %bitcast_add_fusion.3 = f32[3,2,256,256]{3,1,2,0:T(2,128)S(1)} fusion(f32[3,2,256,256]{3,1,2,0:T(2,128)S(1)} %copy-done, f32[3,8,256,256]{3,1,2,0:T(8,128)} %copy.94, pred[8]{0:T(512)(128)(4,1)S(1)} %compare_and_fusion.7, s32[8]{0:T(128)S(1)} %dynamic_slice.46, s32[2]{0:T(128)S(1)} %get-tuple-element.265), kind=kOutput, calls=%fused_computation.8.clone.clone.1 | convolution fusion | flops 38141984 | bytes 9437232 | tf_op jit(solution)/shard_map/while/body/ks,tkac->tsac/dot_general | solution.py:78
  98.3 1.1 copy-done.1
  99.4 2.7 copy.50
  102.4 309.0 %all-reduce.5.cloned.1.call-done = f32[3,2,256,256]{3,2,1,0:T(8,128)} async-done(((f32[3,2,256,256]{3,2,1,0:T(8,128)}), f32[3,2,256,256]{3,2,1,0:T(8,128)}) %all-reduce.5.cloned.1.call-update) | async-done | bytes 1572880 | tf_op jit(solution)/shard_map/psum | solution.py:87
  411.4 1.1 fusion.33
  412.8 1.3 fusion.24
  414.9 1.0 convolution_bitcast_fusion.8
  415.9 1.3 convolution_add_fusion.1
  417.7 0.8 pad_maximum_fusion.2
  418.5 0.9 pad_maximum_fusion.1
  419.5 1.2 fusion.80
  421.1 0.7 fusion.56
  421.8 56.0 %all-reduce.7.cloned.1.call-done = (f32[3,256,256]{1,2,0:T(8,128)}, f32[1,256,256]{1,2,0:T(8,128)}, f32[2,256,256]{1,2,0:T(8,128)}) async-done(((f32[3,256,256]{1,2,0:T(8,128)}, f32[1,256,256]{1,2,0:T(8,128)}, f32[2,256,256]{1,2,0:T(8,128)}), (f32[3,256,256]{1,2,0:T(8,128)}, f32[1,256,256]{1,2,0:T(8,128)}, f32[2,256,256]{1,2,0:T(8,128)})) %all-reduce.7.cloned.1.call-update) | async-done | bytes 1572880 | tf_op jit(solution)/shard_map/psum | solution.py:111
  477.8 1.1 sub.38
  481.7 2.0 copy.68
  (71 shorter events, 8.6 us)
Async XLA Ops:
  7.2 404.2 %all-reduce.5.cloned.1.call-start = ((), (), s32[]{:S(2)}) async-start(), calls=%async_computation | async-start | bytes 3145728 | tf_op jit(solution)/shard_map/psum | solution.py:87
  7.2 2.7 collective-permute-start
  11.1 22.2 %copy-start.7 = (s32[16]{0:T(128)S(1)}, s32[16]{0:T(128)}, u32[]{:S(2)}) copy-start(s32[16]{0:T(128)} %param.14) | copy-start | bytes 196
  11.1 19.6 %collective-permute-start.1 = (bf16[3,2,256,256]{3,2,1,0:T(8,128)(2,1)S(1)}, bf16[3,2,256,256]{3,2,1,0:T(8,128)(2,1)S(1)}, u32[]{:S(2)}, u32[]{:S(2)}) collective-permute-start(bf16[3,2,256,256]{3,2,1,0:T(8,128)(2,1)S(1)} %broadcast_select_fusion), channel_id=1, source_target_pairs={{0,8},{4,12},{8,0},{12,4},{16,24},{20,28},{24,16},{28,20},{1,9},{5... | collective-permute-start | bytes 2359304 | tf_op jit(solution)/shard_map/ppermute | solution.py:13
  30.8 17.9 %collective-permute-start.2 = (bf16[3,2,256,256]{3,2,1,0:T(8,128)(2,1)S(1)}, bf16[3,2,256,256]{3,2,1,0:T(8,128)(2,1)S(1)}, u32[]{:S(2)}, u32[]{:S(2)}) collective-permute-start(bf16[3,2,256,256]{3,2,1,0:T(8,128)(2,1)S(1)} %broadcast_select_fusion.1), channel_id=1, source_target_pairs={{0,16},{4,20},{8,24},{12,28},{16,0},{20,4},{24,8},{28,12},{1,17},{... | collective-permute-start | bytes 2359304 | tf_op jit(solution)/shard_map/ppermute | solution.py:13
  34.1 16.1 %copy-start.6 = (s32[2,2]{1,0:T(2,128)}, s32[2,2]{1,0:T(2,128)S(1)}, u32[]{:S(2)}) copy-start(s32[2,2]{1,0:T(2,128)S(1)} %gather_fusion.1) | copy-start | bytes 52
  50.2 1.6 copy-start.8
  50.2 1.6 copy-start.9
  59.2 7.6 %copy-start = (f32[3,2,256,256]{3,1,2,0:T(2,128)S(1)}, f32[3,2,256,256]{3,1,2,0:T(2,128)}, u32[]{:S(2)}) copy-start(f32[3,2,256,256]{3,1,2,0:T(2,128)} %get-tuple-element.243) | copy-start | bytes 4718596 | tf_op jit(solution)/shard_map/while
  74.4 1.1 copy-start.1
  83.1 7.6 %copy-start = (f32[3,2,256,256]{3,1,2,0:T(2,128)S(1)}, f32[3,2,256,256]{3,1,2,0:T(2,128)}, u32[]{:S(2)}) copy-start(f32[3,2,256,256]{3,1,2,0:T(2,128)} %get-tuple-element.243) | copy-start | bytes 4718596 | tf_op jit(solution)/shard_map/while
  98.3 1.1 copy-start.1
  102.2 310.3 %copy-start.2 = (bf16[3,2,256,256]{3,2,1,0:T(8,128)(2,1)S(1)}, bf16[3,2,256,256]{3,2,1,0:T(8,128)(2,1)}, u32[]{:S(2)}) copy-start(bf16[3,2,256,256]{3,2,1,0:T(8,128)(2,1)} %param.15) | copy-start | bytes 2359300
  102.2 310.6 %copy-start.3 = (bf16[3,3,256,256]{3,2,1,0:T(8,128)(2,1)S(1)}, bf16[3,3,256,256]{3,2,1,0:T(8,128)(2,1)}, u32[]{:S(2)}) copy-start(bf16[3,3,256,256]{3,2,1,0:T(8,128)(2,1)} %param.16) | copy-start | bytes 3538948
  102.2 375.6 %all-reduce.7.cloned.1.call-start = ((), (), s32[]{:S(2)}) async-start(), calls=%async_computation.1 | async-start | bytes 3145728 | tf_op jit(solution)/shard_map/psum | solution.py:111
  477.8 1.2 copy-start.5
  477.8 1.5 copy-start.4
Sparse Core Ops, SparseCore 0:
  102.3 309.0 all-reduce.4
  419.6 58.1 all-reduce.6
where the time goes:
time: 493 us; the launch traced here: 490 us
  waiting for transfers between devices  398 us (81%)
  matrix products  32.9 us (7%)
  local copies, waits for them, and re-layouts  29.2 us (6%)
  between operations  15 us (3%)
  other arithmetic  9.31 us (2%)
  starting transfers between devices  5.56 us (1%)
    psum x1, waiting for transfers between devices, per_device(): base_part = lax.psum(partial_value, 'col')  309 us
    psum x1, waiting for transfers between devices, per_device(): summed = lax.psum(jnp.stack(term_list), 'row')  56 us
    ppermute x3, waiting for transfers between devices, partner_2(): return lax.ppermute(value, axis, pairs)  33.4 us
    dot_general x2, matrix products, accumulate(): jnp.einsum('ks,tkac->tsac', target, products, precision=exact_mode)  15.2 us
    transpose x2, local copies, waits for them, and re-layouts, accumulate(): jnp.einsum('kab,skbc->skac', block_part, factors, preferred_element_type=...  13.6 us
    dot_general x2, matrix products, accumulate(): jnp.einsum('kab,skbc->skac', block_part, factors, preferred_element_type=...  10.2 us
  transfers between devices with their start and end apart: 5, of which 5 were waited for; matrix products, arithmetic and copies ran while one was open for 1% of the time, Pallas kernels for 0%

commit v1 on v0

--- a/solution.py
+++ b/solution.py
@@ -84,7 +84,7 @@
         jnp.zeros((supernodes, slot_count, block_width, block_width), jnp.float32),
     )
     share_rows = block_width // col_devs
-    base_part = lax.psum(partial_value, "col")
+    base_part = jnp.sum(jax.lax.all_gather(partial_value, "col"), 0)
     lower_links = lower_new.astype(jnp.float32)
     panels = []
     blocks_new = {}

time: 493 us -> 541 us (1.097)
  waiting for transfers between devices: 398 us -> 444 us
    all_gather x0 -> x1, waiting for transfers between devices: none -> 355 us  [per_device(): base_part = jnp.sum(jax.lax.all_gather(partial_value, 'col'), 0)]
    psum x1 -> x0, waiting for transfers between devices: 309 us -> none  [per_device(): base_part = lax.psum(partial_value, 'col')]
  transfers between devices with their start and end apart: 5 -> 5, of which waited for: 5 -> 5; matrix products, arithmetic and copies ran while one was open for 1% -> 0% of each run, Pallas kernels for 0% -> 0%
where the time goes in v1:
time: 541 us; the launch traced here: 539 us
  waiting for transfers between devices  444 us (82%)
  matrix products  33.5 us (6%)
  local copies, waits for them, and re-layouts  28.6 us (5%)
  between operations  15 us (3%)
  other arithmetic  11.7 us (2%)
  starting transfers between devices  5.56 us (1%)
    all_gather x1, waiting for transfers between devices, per_device(): base_part = jnp.sum(jax.lax.all_gather(partial_value, 'col'), 0)  355 us
    psum x1, waiting for transfers between devices, per_device(): summed = lax.psum(jnp.stack(term_list), 'row')  55.7 us
    ppermute x3, waiting for transfers between devices, partner_2(): return lax.ppermute(value, axis, pairs)  33.4 us
    dot_general x2, matrix products, accumulate(): jnp.einsum('ks,tkac->tsac', target, products, precision=exact_mode)  15.2 us
    transpose x2, local copies, waits for them, and re-layouts, accumulate(): jnp.einsum('kab,skbc->skac', block_part, factors, preferred_element_type=...  13.6 us
  transfers between devices with their start and end apart: 5, of which 5 were waited for; matrix products, arithmetic and copies ran while one was open for 0% of the time, Pallas kernels for 0%

profile of v1, /device:TPU:0, one launch (start us, length us, event | category | flops | bytes accessed | tf_op | source)
XLA Modules:
  0.0 538.9 jit_solution(14985960354779314915)
XLA Ops:
  7.8 2.1 collective-permute-done
  9.9 1.2 broadcast_select_fusion
  11.1 2.9 collective-permute-start.1
  14.0 16.7 %collective-permute-done.1 = bf16[3,2,256,256]{3,2,1,0:T(8,128)(2,1)S(1)} collective-permute-done((bf16[3,2,256,256]{3,2,1,0:T(8,128)(2,1)S(1)}, bf16[3,2,256,256]{3,2,1,0:T(8,128)(2,1)S(1)}, u32[]{:S(2)}, u32[]{:S(2)}) %collective-permute-start.1) | collective-permute-done | bytes 786464 | tf_op jit(solution)/shard_map/ppermute | solution.py:13
  30.8 1.8 collective-permute-start.2
  34.2 14.6 %collective-permute-done.2 = bf16[3,2,256,256]{3,2,1,0:T(8,128)(2,1)S(1)} collective-permute-done((bf16[3,2,256,256]{3,2,1,0:T(8,128)(2,1)S(1)}, bf16[3,2,256,256]{3,2,1,0:T(8,128)(2,1)S(1)}, u32[]{:S(2)}, u32[]{:S(2)}) %collective-permute-start.2) | collective-permute-done | bytes 786464 | tf_op jit(solution)/shard_map/ppermute | solution.py:13
  48.8 1.4 maximum_select_fusion
  50.2 1.5 broadcast_in_dim.31
  51.7 47.7 %while.12 = (s32[]{:T(128)}, f32[3,2,256,256]{3,1,2,0:T(2,128)}, s32[]{:T(128)}, s32[96]{0:T(128)S(1)}, s32[2,2]{1,0:T(2,128)}, /*index=5*/bf16[3,4,256,256]{3,2...) while((s32[]{:T(128)}, f32[3,2,256,256]{3,1,2,0:T(2,128)}, ...), condition=%wide.wide.region_3.4_spmd.clone, body=%wide.wide.region_0.3_spmd.clone.sunk | while | flops 845022464 | bytes 51385088 | solution.py:80
  51.9 2.2 gather_fusion
  54.1 5.1 fusion.112
  59.2 6.8 %copy.128 = f32[3,8,256,256]{3,1,2,0:T(8,128)} copy(f32[3,8,256,256]{2,3,0,1:T(8,128)} %fusion.112) | data formatting | bytes 12582912 | tf_op jit(solution)/shard_map/while/body/kab,skbc->skac/transpose | solution.py:74
  66.8 7.6 %bitcast_add_fusion.3 = f32[3,2,256,256]{3,1,2,0:T(2,128)S(1)} fusion(f32[3,2,256,256]{3,1,2,0:T(2,128)S(1)} %copy-done, f32[3,8,256,256]{3,1,2,0:T(8,128)} %copy.128, pred[8]{0:T(512)(128)(4,1)S(1)} %compare_and_fusion.7, s32[8]{0:T(128)S(1)} %dynamic_slice.46, s32[2]{0:T(128)S(1)} %get-tuple-element.267), kind=kOutput, calls=%fused_computation.8.clone.clone.1 | convolution fusion | flops 38141984 | bytes 9437232 | tf_op jit(solution)/shard_map/while/body/ks,tkac->tsac/dot_general | solution.py:78
  74.4 1.1 copy-done.1
  75.8 2.2 gather_fusion
  77.9 5.1 fusion.112
  83.0 6.8 %copy.128 = f32[3,8,256,256]{3,1,2,0:T(8,128)} copy(f32[3,8,256,256]{2,3,0,1:T(8,128)} %fusion.112) | data formatting | bytes 12582912 | tf_op jit(solution)/shard_map/while/body/kab,skbc->skac/transpose | solution.py:74
  90.7 7.6 %bitcast_add_fusion.3 = f32[3,2,256,256]{3,1,2,0:T(2,128)S(1)} fusion(f32[3,2,256,256]{3,1,2,0:T(2,128)S(1)} %copy-done, f32[3,8,256,256]{3,1,2,0:T(8,128)} %copy.128, pred[8]{0:T(512)(128)(4,1)S(1)} %compare_and_fusion.7, s32[8]{0:T(128)S(1)} %dynamic_slice.46, s32[2]{0:T(128)S(1)} %get-tuple-element.267), kind=kOutput, calls=%fused_computation.8.clone.clone.1 | convolution fusion | flops 38141984 | bytes 9437232 | tf_op jit(solution)/shard_map/while/body/ks,tkac->tsac/dot_general | solution.py:78
  98.3 1.1 copy-done.1
  99.4 2.7 copy.73
  102.4 355.3 %all-gather.3.cloned.1.call-done = f32[12,2,256,256]{3,2,1,0:T(8,128)} async-done(((f32[3,2,256,256]{3,2,1,0:T(8,128)}), f32[12,2,256,256]{3,2,1,0:T(8,128)}) %all-gather.3.cloned.1.call-update) | async-done | bytes 6291472 | tf_op jit(solution)/shard_map/all_gather | solution.py:87
  457.7 3.5 reduce_sum.20
  461.5 1.1 fusion.24
  462.6 1.1 convolution_add_fusion.1
  464.6 1.0 convolution_bitcast_fusion.8
  465.5 1.1 fusion.25
  466.9 0.8 pad_maximum_fusion.2
  467.8 0.9 pad_maximum_fusion.1
  469.7 0.7 fusion.56
  470.4 55.7 %all-reduce.4.cloned.1.call-done = (f32[3,256,256]{1,2,0:T(8,128)}, f32[1,256,256]{1,2,0:T(8,128)}, f32[2,256,256]{1,2,0:T(8,128)}) async-done(((f32[3,256,256]{1,2,0:T(8,128)}, f32[1,256,256]{1,2,0:T(8,128)}, f32[2,256,256]{1,2,0:T(8,128)}), (f32[3,256,256]{1,2,0:T(8,128)}, f32[1,256,256]{1,2,0:T(8,128)}, f32[2,256,256]{1,2,0:T(8,128)})) %all-reduce.4.cloned.1.call-update) | async-done | bytes 1572880 | tf_op jit(solution)/shard_map/psum | solution.py:111
  526.2 1.1 sub.38
  530.1 2.0 copy.95
  (74 shorter events, 8.9 us)
Async XLA Ops:
  7.2 450.5 %all-gather.3.cloned.1.call-start = ((), (), s32[]{:S(2)}) async-start(), calls=%async_computation | async-start | bytes 7864320 | tf_op jit(solution)/shard_map/all_gather | solution.py:87
  7.2 2.7 collective-permute-start
  11.1 22.2 %copy-start.8 = (s32[16]{0:T(128)S(1)}, s32[16]{0:T(128)}, u32[]{:S(2)}) copy-start(s32[16]{0:T(128)} %param.14) | copy-start | bytes 196
  11.1 19.6 %collective-permute-start.1 = (bf16[3,2,256,256]{3,2,1,0:T(8,128)(2,1)S(1)}, bf16[3,2,256,256]{3,2,1,0:T(8,128)(2,1)S(1)}, u32[]{:S(2)}, u32[]{:S(2)}) collective-permute-start(bf16[3,2,256,256]{3,2,1,0:T(8,128)(2,1)S(1)} %broadcast_select_fusion), channel_id=1, source_target_pairs={{0,8},{4,12},{8,0},{12,4},{16,24},{20,28},{24,16},{28,20},{1,9},{5... | collective-permute-start | bytes 2359304 | tf_op jit(solution)/shard_map/ppermute | solution.py:13
  30.8 17.9 %collective-permute-start.2 = (bf16[3,2,256,256]{3,2,1,0:T(8,128)(2,1)S(1)}, bf16[3,2,256,256]{3,2,1,0:T(8,128)(2,1)S(1)}, u32[]{:S(2)}, u32[]{:S(2)}) collective-permute-start(bf16[3,2,256,256]{3,2,1,0:T(8,128)(2,1)S(1)} %broadcast_select_fusion.1), channel_id=1, source_target_pairs={{0,16},{4,20},{8,24},{12,28},{16,0},{20,4},{24,8},{28,12},{1,17},{... | collective-permute-start | bytes 2359304 | tf_op jit(solution)/shard_map/ppermute | solution.py:13
  34.1 16.1 %copy-start.7 = (s32[2,2]{1,0:T(2,128)}, s32[2,2]{1,0:T(2,128)S(1)}, u32[]{:S(2)}) copy-start(s32[2,2]{1,0:T(2,128)S(1)} %gather_fusion.1) | copy-start | bytes 52
  50.2 1.6 copy-start.9
  50.2 1.6 copy-start.10
  59.2 7.6 %copy-start = (f32[3,2,256,256]{3,1,2,0:T(2,128)S(1)}, f32[3,2,256,256]{3,1,2,0:T(2,128)}, u32[]{:S(2)}) copy-start(f32[3,2,256,256]{3,1,2,0:T(2,128)} %get-tuple-element.245) | copy-start | bytes 4718596 | tf_op jit(solution)/shard_map/while
  74.4 1.1 copy-start.1
  83.0 7.6 %copy-start = (f32[3,2,256,256]{3,1,2,0:T(2,128)S(1)}, f32[3,2,256,256]{3,1,2,0:T(2,128)}, u32[]{:S(2)}) copy-start(f32[3,2,256,256]{3,1,2,0:T(2,128)} %get-tuple-element.245) | copy-start | bytes 4718596 | tf_op jit(solution)/shard_map/while
  98.3 1.1 copy-start.1
  102.1 424.0 %all-reduce.4.cloned.1.call-start = ((), (), s32[]{:S(2)}) async-start(), calls=%async_computation.1 | async-start | bytes 3145728 | tf_op jit(solution)/shard_map/psum | solution.py:111
  457.7 3.5 copy-start.2
  467.8 1.4 copy-start.4
  469.5 57.8 %copy-start.3 = (bf16[3,3,256,256]{3,2,1,0:T(8,128)(2,1)S(1)}, bf16[3,3,256,256]{3,2,1,0:T(8,128)(2,1)}, u32[]{:S(2)}) copy-start(bf16[3,3,256,256]{3,2,1,0:T(8,128)(2,1)} %param.16) | copy-start | bytes 3538948
  526.2 1.2 copy-start.6
  526.2 1.5 copy-start.5
Sparse Core Ops, SparseCore 0:
  102.3 355.3 all-gather.2
  468.9 57.2 all-reduce.3
